TPU v7x, 512 devices: a whole 4x8x8 slice. The times are simulated.
512 devices in a mesh: seq: 16 (over y, core), kv: 8 (over z), dp: 4 (over x).
Axes of the slice: x: 4, y: 8, z: 8, core: 2. Of those that a mesh axis runs over, the one named last changes fastest.
Arguments:
- queries: bfloat16 [65536, 2048], P(('dp', 'seq', 'kv')), parts along dimension 0, may hold values from -9 to 9
- keys: bfloat16 [65536, 512], P(('dp', 'seq', 'kv')), parts along dimension 0, may hold values from -4 to 4
- values: bfloat16 [65536, 512], P(('dp', 'seq', 'kv')), parts along dimension 0, may hold values from -6 to 6
- doc_ids: int32 [65536], P(('dp', 'seq', 'kv')), parts along dimension 0, may hold values from 0 to 7, never falling along the last dimension, each value on 1 to 4096 neighbouring positions
- beta: float32 [16], replicated, may hold values from -2 to 2
- lin_gain: float32 [2048], replicated, may hold values from 0.1 to 1.9
Outputs:
- mixed: float32 [65536, 2048], P(('dp', 'seq', 'kv')), parts along dimension 0
There are 4 independent parts, one for each index of `dp`. A program takes and returns all parts, laid end to end along the dimension named above; an argument that names none is the same for every part. Nothing has to cross between parts.
Inputs may be any that keep to these rules, and one draw needn't show every extreme that they name: `doc_ids`: document ids never fall along a packed sequence; each document holds 1 to 4096 tokens.
All inputs are finite; a program needn't handle non-finite values.
Results may differ from a plain program's by a relative error of at most 0.0012.
Values may be sent and summed in bfloat16 or wider, within the bound.
A program may use at most 64 MiB of HBM per device.

v0:
```python
import jax
import jax.numpy as jnp
from jax import lax
from jax.sharding import Mesh
from jax.sharding import PartitionSpec as P

HEADS = 16
KV_HEADS = 4
HEAD_DIM = 128
SEQ = ("seq_0", "seq_1")
DP_SEQ_KV = ("dp", "seq_0", "seq_1", "kv")


def in_one_piece(arrays, axis, dim, along):
    widths = [a.shape[along] for a in arrays]
    both = jnp.concatenate(arrays, axis=along)
    out = lax.all_gather(both, axis, axis=dim, tiled=True)
    return tuple(jnp.split(out, [sum(widths[:k]) for k in range(1, len(widths))], axis=along))


def nothing_yet(x, identity):
    return jax.tree.map(
        lambda part, zero: jnp.zeros_like(part) + jnp.asarray(zero, part.dtype), x, identity
    )


def all_in_one(x, axis):
    leaves = jax.tree.leaves(x)
    order = sorted(range(len(leaves)), key=lambda k: -leaves[k].size)
    width = (1, *leaves[order[0]].shape)[-1]
    lines = [
        jnp.pad(leaves[k].reshape(-1), (0, -leaves[k].size % width)).reshape(-1, width)
        for k in order
    ]
    both, at, found = (lax.all_gather(jnp.concatenate(lines), axis), 0, {})
    for k, line in zip(order, lines):
        section = both[:, at : at + len(line)].reshape(len(both), -1)
        found[k] = section[:, : leaves[k].size].reshape(-1, *leaves[k].shape)
        at += len(line)
    numbers = iter(range(len(leaves)))
    return jax.tree.map(lambda _: found[next(numbers)], x)


def collected_alike(x, axis):
    leaves, found = (jax.tree.leaves(x), {})
    for initial, a in enumerate(leaves):
        if initial not in found:
            alike = [k for k, b in enumerate(leaves) if b.dtype == a.dtype]
            got = (
                all_in_one([leaves[k] for k in alike], axis)
                if len(alike) > 1
                else [lax.all_gather(a, axis)]
            )
            for k, b in zip(alike, got):
                found[k] = b
    numbers = iter(range(len(leaves)))
    return jax.tree.map(lambda _: found[next(numbers)], x)


def prefix_by_axis(x, axes, combine, identity):
    before = start = nothing_yet(x, identity)
    so_far = x
    for axis in reversed(axes):
        size, here = (lax.axis_size(axis), lax.axis_index(axis))
        pieces = collected_alike(so_far, axis)
        inside, so_far = (start, start)
        for k in range(size):
            passed = k < here
            so_far = combine(so_far, jax.tree.map(lambda part: part[k], pieces))
            inside = jax.tree.map(lambda new, old: jnp.where(passed, new, old), so_far, inside)
        before = combine(inside, before)
    return before


def join_states(earlier, later):
    state_early, first_early, last_early = earlier
    state_late, first_late, last_late = later
    empty_late = first_late < 0
    joined = (first_late == last_late) & (last_early == first_late)
    merged = state_late + jnp.where(joined, state_early, jnp.zeros_like(state_early))
    combined = jnp.where(empty_late, state_early, merged)
    first_doc = jnp.where(first_early < 0, first_late, first_early)
    last_doc = jnp.where(empty_late, last_early, last_late)
    return (combined, first_doc, last_doc)


def tail_merge(one_side, other_side):
    state_one, first_one, last_one = one_side
    state_other, first_other, last_other = other_side
    top_doc = jnp.maximum(last_one, last_other)
    state_sum = jnp.where(last_one == top_doc, state_one, jnp.zeros_like(state_one))
    state_sum = state_sum + jnp.where(
        last_other == top_doc, state_other, jnp.zeros_like(state_other)
    )
    return (state_sum, jnp.minimum(first_one, first_other), top_doc)


def tail_state(key_rows, value_rows, doc_rows, target_doc):
    count = key_rows.shape[0]
    key_heads = key_rows.reshape(count, KV_HEADS, HEAD_DIM)
    value_heads = value_rows.reshape(count, KV_HEADS, HEAD_DIM)
    live = doc_rows == target_doc
    masked = jnp.where(live[:, None, None], key_heads, jnp.zeros_like(key_heads))
    return jnp.einsum("rgd,rge->gde", masked, value_heads, preferred_element_type=jnp.float32)


def attend_block(
    carry, query_heads, query_pos, query_doc, key_rows, value_rows, key_doc, key_start
):
    running_max, running_sum, accumulated = carry
    key_count = key_rows.shape[0]
    key_heads = key_rows.reshape(key_count, KV_HEADS, HEAD_DIM)
    value_heads = value_rows.reshape(key_count, KV_HEADS, HEAD_DIM)
    scores = jnp.einsum(
        "rgqd,kgd->gqrk", query_heads, key_heads, preferred_element_type=jnp.float32
    )
    scores = scores / jnp.sqrt(jnp.float32(HEAD_DIM))
    key_pos = key_start + jnp.arange(key_count, dtype=jnp.int32)
    allowed = (key_pos[None, :] <= query_pos[:, None]) & (key_doc[None, :] == query_doc[:, None])
    masked = jnp.where(allowed, scores, jnp.float32(-1e30))
    new_max = jnp.maximum(running_max, jnp.max(masked, axis=-1))
    factor = jnp.exp(running_max - new_max)
    weights = jnp.where(allowed, jnp.exp(masked - new_max[..., None]), jnp.float32(0.0))
    new_sum = running_sum * factor + jnp.sum(weights, axis=-1)
    product = jnp.einsum(
        "gqrk,kge->gqre",
        weights.astype(jnp.bfloat16),
        value_heads,
        preferred_element_type=jnp.float32,
    )
    new_accum = accumulated * factor[..., None] + product
    return (new_max, new_sum, new_accum)


def on_device(queries, keys, values, doc_ids, beta, lin_gain):
    row_count = queries.shape[0]
    groups = HEADS // KV_HEADS
    query_heads = queries.reshape(row_count, KV_HEADS, groups, HEAD_DIM)
    position = lax.axis_index("kv") * row_count
    query_pos = position + jnp.arange(row_count, dtype=jnp.int32)
    last_query = position + row_count - 1
    initial = (
        jnp.full((KV_HEADS, groups, row_count), -1e30, jnp.float32),
        jnp.zeros((KV_HEADS, groups, row_count), jnp.float32),
        jnp.zeros((KV_HEADS, groups, row_count, HEAD_DIM), jnp.float32),
    )
    empty_tail = (
        jnp.zeros((KV_HEADS, HEAD_DIM, HEAD_DIM), jnp.float32),
        jnp.array(2**30, jnp.int32),
        jnp.array(-1, jnp.int32),
    )
    key_piece, value_piece, doc_piece = (
        *in_one_piece((keys, values), "kv", 0, 1),
        lax.all_gather(doc_ids, "kv", axis=0, tiled=True),
    )
    blocks = key_piece.shape[0] // row_count

    def one_block(state, item):
        soft_state, tail_now = state
        key_block, value_block, doc_block, number = item
        block_start = number * row_count
        soft_next = lax.cond(
            block_start <= last_query,
            lambda inner: attend_block(
                inner,
                query_heads,
                query_pos,
                doc_ids,
                key_block,
                value_block,
                doc_block,
                block_start,
            ),
            lambda inner: inner,
            soft_state,
        )
        block_tail = (
            tail_state(key_block, value_block, doc_block, doc_block[-1]),
            doc_block[0],
            doc_block[-1],
        )
        tail_now = tail_merge(tail_now, block_tail)
        return ((soft_next, tail_now), None)

    stacked = (
        key_piece.reshape(blocks, row_count, -1),
        value_piece.reshape(blocks, row_count, -1),
        doc_piece.reshape(blocks, row_count),
        jnp.arange(blocks, dtype=jnp.int32),
    )
    result, _ = lax.scan(one_block, (initial, empty_tail), stacked)
    running, segment_tail = result
    running_max, running_sum, accumulated = running
    soft_out = jnp.transpose(accumulated / running_sum[..., None], (2, 0, 1, 3))
    identity = (
        jnp.zeros((KV_HEADS, HEAD_DIM, HEAD_DIM), jnp.float32),
        jnp.array(-1, jnp.int32),
        jnp.array(-1, jnp.int32),
    )
    memory = prefix_by_axis(segment_tail, SEQ, join_states, identity)
    memory_state, memory_first, memory_last = memory
    query_float = query_heads.astype(jnp.float32)
    recalled = jnp.einsum(
        "rgqd,gde->rgqe", query_float, memory_state, precision=lax.Precision.HIGHEST
    )
    recalled = jnp.where((doc_ids == memory_last)[:, None, None, None], recalled, jnp.float32(0.0))
    mean_square = jnp.mean(recalled * recalled, axis=-1, keepdims=True)
    normed = (
        recalled * lax.rsqrt(mean_square + 1e-06) * lin_gain.reshape(KV_HEADS, groups, HEAD_DIM)
    )
    mixing = jax.nn.sigmoid(beta).reshape(KV_HEADS, groups)[None, :, :, None]
    mixed = mixing * normed + (1.0 - mixing) * soft_out
    return mixed.reshape(row_count, HEADS * HEAD_DIM).astype(jnp.float32)


def solution(mesh):
    split = Mesh(
        mesh.devices.reshape(8, 2, mesh.shape["kv"], mesh.shape["dp"]),
        ("seq_0", "seq_1", "kv", "dp"),
    )
    in_specs = (P(DP_SEQ_KV, None), P(DP_SEQ_KV, None), P(DP_SEQ_KV, None), P(DP_SEQ_KV), P(), P())
    out_specs = P(DP_SEQ_KV, None)
    return jax.shard_map(
        on_device, mesh=split, in_specs=in_specs, out_specs=out_specs, check_vma=False
    )
```

profile of v0, /device:TPU:2, one launch (start us, length us, event | category | flops | bytes accessed | tf_op | source)
XLA Modules:
  0.0 181.8 jit_solution(15142142390558384804)
XLA Ops:
  6.5 1.7 pad_maximum_fusion
  8.3 1.3 copy.45
  10.0 1.3 dynamic-slice
  11.9 22.2 %all-gather.3 = s32[8,1,128]{2,1,0:T(1,128)S(1)} all-gather(s32[1,1,128]{2,1,0:T(1,128)S(1)} %bitcast.210), channel_id=1, replica_groups=mesh['seq_0'=8,'seq_1'=2,'kv'=8,'dp'=4] {'kv'}, dimensions={0}, use_global_device_ids=true | all-gather | bytes 4608 | tf_op jit(solution)/shard_map/all_gather | solution.py:154
  34.1 24.7 %all-gather.7.cloned.1.call-done = bf16[1024,1024]{1,0:T(8,128)(2,1)} async-done(((bf16[128,1024]{1,0:T(8,128)(2,1)}), bf16[1024,1024]{1,0:T(8,128)(2,1)}) %all-gather.7.cloned.1.call-update) | async-done | bytes 2097168 | tf_op jit(solution)/shard_map/all_gather | solution.py:17
  58.8 2.6 %fusion.103 = (bf16[1024,512]{1,0:T(8,128)(2,1)S(1)}, bf16[1024,512]{1,0:T(8,128)(2,1)}) fusion(bf16[1024,1024]{1,0:T(8,128)(2,1)} %all-gather.7.cloned.1.call-done), kind=kLoop, calls=%fused_computation.128 | loop fusion | bytes 4194304 | tf_op jit(solution)/shard_map/split | solution.py:18
  61.5 48.8 %while.21 = (s32[]{:T(128)}, f32[4,4,128]{2,1,0:T(4,128)S(1)}, f32[4,4,128]{2,1,0:T(4,128)S(1)}, f32[4,4,128,128]{3,2,1,0:T(8,128)S(1)}, f32[4,128,128]{2,1,0:T(...) while((s32[]{:T(128)}, f32[4,4,128]{2,1,0:T(4,128)S(1)}, ...), condition=%wide.region_5.6_spmd.clone, body=%wide.region_0.5_spmd.clone.sunk | while | flops 154259840 | bytes 8067273 | solution.py:191
  61.6 0.6 dynamic_slice.31
  62.8 0.9 constant_dynamic-slice_fusion.6
  64.0 1.5 conditional.3
  64.8 0.7 convolution_add_fusion
  65.5 0.6 fusion.117
  66.1 0.6 compare_bitcast_fusion.2
  68.9 0.6 dynamic_slice.31
  70.2 0.9 constant_dynamic-slice_fusion.6
  71.4 0.6 fusion.117
  72.0 0.6 compare_bitcast_fusion.2
  74.8 0.6 dynamic_slice.31
  76.1 0.9 constant_dynamic-slice_fusion.6
  77.3 0.6 fusion.117
  77.9 0.6 compare_bitcast_fusion.2
  80.7 0.6 dynamic_slice.31
  82.0 0.9 constant_dynamic-slice_fusion.6
  83.2 0.6 fusion.117
  83.9 0.6 compare_bitcast_fusion.2
  86.7 0.6 dynamic_slice.31
  87.9 0.9 constant_dynamic-slice_fusion.6
  89.2 0.6 fusion.117
  89.8 0.6 compare_bitcast_fusion.2
  92.6 0.6 dynamic_slice.31
  93.8 0.9 constant_dynamic-slice_fusion.6
  95.7 0.6 compare_bitcast_fusion.2
  98.5 0.6 dynamic_slice.31
  99.8 0.9 constant_dynamic-slice_fusion.6
  101.6 0.6 compare_bitcast_fusion.2
  104.4 0.6 dynamic_slice.31
  105.7 0.9 constant_dynamic-slice_fusion.6
  107.5 0.6 compare_bitcast_fusion.2
  110.5 2.3 %all-gather.2 = f32[8,128,128]{2,1,0:T(8,128)S(1)} all-gather(f32[4,128,128]{2,1,0:T(8,128)S(1)} %get-tuple-element.130), channel_id=4, replica_groups=mesh['seq_0'=8,'seq_1'=2,'kv'=8,'dp'=4] {'seq_1'}, dimensions={0}, use_global_device_ids=true | all-gather | bytes 786432 | tf_op jit(solution)/shard_map/all_gather | solution.py:52
  112.8 1.8 all-reduce
  114.7 0.7 fusion.105
  119.2 0.7 fusion.34
  120.0 1.2 dynamic-slice.1
  124.9 13.5 %all-reduce.1 = s32[16]{0:T(128)S(1)} all-reduce(s32[16]{0:T(128)S(1)} %fusion.99), channel_id=3, replica_groups=mesh['seq_0'=8,'seq_1'=2,'kv'=8,'dp'=4] {'seq_0'}, use_global_device_ids=true, to_apply=%add.1 | all-reduce | flops 16 | bytes 128
  138.5 0.7 fusion.104
  161.4 9.1 %all-gather.9.cloned.1.call-done = f32[8,4,128,128]{3,2,1,0:T(8,128)} async-done(((f32[1,4,128,128]{3,2,1,0:T(8,128)}), f32[8,4,128,128]{3,2,1,0:T(8,128)}) %all-gather.9.cloned.1.call-update) | async-done | bytes 2097168 | tf_op jit(solution)/shard_map/all_gather | solution.py:52
  170.5 2.6 %multiply_reduce_fusion = (f32[128,4,4]{0,2,1:T(4,128)S(1)}, f32[128,4,4,128]{0,3,2,1:T(8,128)S(1)}) fusion(bf16[128,4,4,128]{0,3,2,1:T(8,128)(2,1)S(1)} %bitcast.203, f32[8,4,128,128]{3,2,1,0:T(8,128)} %all-gather.9.cloned.1.call-done, f32[8,128,128]{2,1,0:T(8,128)S(1)} %all-gather.2, pred[]{:T(512)S(6)} %lt.43, pred[]{:T(512)S(6)} %and.43, pred[]{:T(512)S(6)} %gt.31, ...), kind=kOutput, calls=%fused_computation.31 | convolution fusion | flops 405993472 | bytes 4202654 | tf_op jit(solution)/shard_map/rgqd,gde->rgqe/dot_general | solution.py:203
  173.6 1.3 copy.52
  (90 shorter events, 8.4 us)
Async XLA Ops:
  6.5 5.3 %copy-start.2 = (s32[128]{0:T(128)S(1)}, s32[128]{0:T(128)}, u32[]{:S(2)}) copy-start(s32[128]{0:T(128)} %param.13) | copy-start | bytes 1540
  6.5 52.2 %all-gather.7.cloned.1.call-start = ((), (), s32[]{:S(2)}) async-start(), calls=%async_computation | async-start | bytes 2359296 | tf_op jit(solution)/shard_map/all_gather | solution.py:17
  8.3 162.2 %all-gather.9.cloned.1.call-start = ((), (), s32[]{:S(2)}) async-start(), calls=%async_computation.1 | async-start | bytes 2359296 | tf_op jit(solution)/shard_map/all_gather | solution.py:52
  9.7 51.8 %copy-start = (bf16[128,2048]{0,1:T(8,128)(2,1)}, bf16[128,2048]{0,1:T(8,128)(2,1)S(1)}, u32[]{:S(2)}) copy-start(bf16[128,2048]{0,1:T(8,128)(2,1)S(1)} %copy.45) | copy-start | bytes 1572868
  61.5 60.2 %copy-start.4 = (f32[16]{0:T(128)S(1)}, f32[16]{0:T(128)}, u32[]{:S(2)}) copy-start(f32[16]{0:T(128)} %param.14) | copy-start | bytes 196
  110.5 60.0 %copy-start.1 = (bf16[128,2048]{0,1:T(8,128)(2,1)S(1)}, bf16[128,2048]{0,1:T(8,128)(2,1)}, u32[]{:S(2)}) copy-start(bf16[128,2048]{0,1:T(8,128)(2,1)} %copy-done) | copy-start | bytes 1572868
  161.3 11.8 %copy-start.3 = (f32[2048]{0:T(1024)S(1)}, f32[2048]{0:T(1024)}, u32[]{:S(2)}) copy-start(f32[2048]{0:T(1024)} %param.15) | copy-start | bytes 24580
Sparse Core Ops, SparseCore 0:
  9.4 49.2 all-gather.6
  120.1 50.3 all-gather.8
where the time goes:
time: 183 us; the launch traced here: 182 us
  between operations  43.2 us (24%)
  blocking collectives  39.9 us (22%)
  waiting for transfers between devices  33.8 us (18%)
  local copies, waits for them, and re-layouts  29.4 us (16%)
  loops' own time  21.2 us (12%)
  other arithmetic  8.77 us (5%)
  matrix products  5.49 us (3%)
    all_gather x1, waiting for transfers between devices, in_one_piece(): out = lax.all_gather(both, axis, axis=dim, tiled=True)  24.7 us
    all_gather x1, blocking collectives, on_device(): lax.all_gather(doc_ids, 'kv', axis=0, tiled=True)  22.2 us
    another operation x1, loops' own time, on_device(): result, _ = lax.scan(one_block, (initial, empty_tail), stacked)  21 us
    unnamed x2, blocking collectives  15.3 us
    dynamic_slice x40, local copies, waits for them, and re-layouts, on_device(): result, _ = lax.scan(one_block, (initial, empty_tail), stacked)  14.4 us
    all_gather x1, waiting for transfers between devices, collected_alike(): lax.all_gather(a, axis)  9.14 us
    eq x8, other arithmetic, tail_state(): live = doc_rows == target_doc  5.13 us
    slice x8, local copies, waits for them, and re-layouts, one_block(): doc_block[0]  4.86 us
  transfers between devices with their start and end apart: 2, of which 2 were waited for; matrix products, arithmetic and copies ran while one was open for 3% of the time, Pallas kernels for 0%

commit v1 on v0

--- a/solution.py
+++ b/solution.py
@@ -151,7 +151,9 @@
     )
     key_piece, value_piece, doc_piece = (
         *in_one_piece((keys, values), "kv", 0, 1),
-        lax.all_gather(doc_ids, "kv", axis=0, tiled=True),
+        jnp.concatenate(
+            lax.all_to_all(jnp.stack([doc_ids] * lax.axis_size("kv")), "kv", 0, 0), axis=0
+        ),
     )
     blocks = key_piece.shape[0] // row_count
 

time: 183 us -> 183 us (level)
  blocking collectives: 39.9 us -> 17.6 us
  waiting for transfers between devices: 33.8 us -> 44.3 us
  starting transfers between devices: 0.04 us -> 10.4 us
  local copies, waits for them, and re-layouts: 29.4 us -> 31.4 us
    all_gather x1 -> x0, blocking collectives: 22.2 us -> none  [on_device(): lax.all_gather(doc_ids, 'kv', axis=0, tiled=True)]
    all_gather x1, waiting for transfers between devices: 24.7 us -> 35.2 us  [in_one_piece(): out = lax.all_gather(both, axis, axis=dim, tiled=True)]
    all_to_all x0 -> x1, starting transfers between devices: none -> 10.3 us  [on_device(): lax.all_to_all(jnp.stack([doc_ids] * lax.axis_size('kv')), 'kv', 0, 0)]
  transfers between devices with their start and end apart: 2 -> 3, of which waited for: 2 -> 2; matrix products, arithmetic and copies ran while one was open for 3% -> 5% of each run, Pallas kernels for 0% -> 0%
where the time goes in v1:
time: 183 us; the launch traced here: 182 us
  waiting for transfers between devices  44.3 us (24%)
  between operations  43.1 us (24%)
  local copies, waits for them, and re-layouts  31.4 us (17%)
  loops' own time  20.9 us (11%)
  blocking collectives  17.6 us (10%)
  starting transfers between devices  10.4 us (6%)
  other arithmetic  8.66 us (5%)
  matrix products  5.49 us (3%)
    all_gather x1, waiting for transfers between devices, in_one_piece(): out = lax.all_gather(both, axis, axis=dim, tiled=True)  35.2 us
    another operation x1, loops' own time, on_device(): result, _ = lax.scan(one_block, (initial, empty_tail), stacked)  20.7 us
    unnamed x2, blocking collectives  15.3 us
    dynamic_slice x40, local copies, waits for them, and re-layouts, on_device(): result, _ = lax.scan(one_block, (initial, empty_tail), stacked)  14.7 us
    all_to_all x1, starting transfers between devices, on_device(): lax.all_to_all(jnp.stack([doc_ids] * lax.axis_size('kv')), 'kv', 0, 0)  10.3 us
    all_gather x1, waiting for transfers between devices, collected_alike(): lax.all_gather(a, axis)  8.97 us
    slice x8, local copies, waits for them, and re-layouts, one_block(): doc_block[0]  5.17 us
    eq x8, other arithmetic, tail_state(): live = doc_rows == target_doc  5.03 us
  transfers between devices with their start and end apart: 3, of which 2 were waited for; matrix products, arithmetic and copies ran while one was open for 5% of the time, Pallas kernels for 0%

profile of v1, /device:TPU:2, one launch (start us, length us, event | category | flops | bytes accessed | tf_op | source)
XLA Modules:
  0.0 181.8 jit_solution(3110608633256792767)
XLA Ops:
  6.5 1.7 pad_maximum_fusion
  8.3 1.2 stack.2
  9.5 10.3 %all-to-all-start = ((s32[8,1,128]{2,1,0:T(1,128)}), s32[8,1,128]{2,1,0:T(1,128)S(1)}, u32[]{:S(2)}, u32[]{:S(2)}) async-start(s32[8,1,128]{2,1,0:T(1,128)} %stack.2), calls=%async_computation | async-start | bytes 8192 | tf_op jit(solution)/shard_map/all_to_all | solution.py:155
  19.9 1.3 copy.45
  21.5 1.3 dynamic-slice
  23.5 35.2 %all-gather.6.cloned.1.call-done = bf16[1024,1024]{1,0:T(8,128)(2,1)} async-done(((bf16[128,1024]{1,0:T(8,128)(2,1)}), bf16[1024,1024]{1,0:T(8,128)(2,1)}) %all-gather.6.cloned.1.call-update) | async-done | bytes 2097168 | tf_op jit(solution)/shard_map/all_gather | solution.py:17
  58.8 2.6 %fusion.103 = (bf16[1024,512]{1,0:T(8,128)(2,1)S(1)}, bf16[1024,512]{1,0:T(8,128)(2,1)}) fusion(bf16[1024,1024]{1,0:T(8,128)(2,1)} %all-gather.6.cloned.1.call-done), kind=kLoop, calls=%fused_computation.128 | loop fusion | bytes 4194304 | tf_op jit(solution)/shard_map/split | solution.py:18
  61.6 49.0 %while.21 = (s32[]{:T(128)}, f32[4,4,128]{2,1,0:T(4,128)S(1)}, f32[4,4,128]{2,1,0:T(4,128)S(1)}, f32[4,4,128,128]{3,2,1,0:T(8,128)S(1)}, f32[4,128,128]{2,1,0:T(...) while((s32[]{:T(128)}, f32[4,4,128]{2,1,0:T(4,128)S(1)}, ...), condition=%wide.region_5.6_spmd.clone, body=%wide.region_0.5_spmd.clone.sunk | while | flops 154259840 | bytes 8067273 | solution.py:193
  61.6 0.7 dynamic_slice.31
  62.9 0.9 constant_dynamic-slice_fusion.6
  64.1 1.5 conditional.3
  64.9 0.7 convolution_add_fusion
  65.5 0.6 fusion.117
  66.2 0.6 compare_bitcast_fusion.2
  69.0 0.7 dynamic_slice.31
  70.3 0.9 constant_dynamic-slice_fusion.6
  71.5 0.6 fusion.117
  72.1 0.6 compare_bitcast_fusion.2
  74.9 0.7 dynamic_slice.31
  76.2 0.9 constant_dynamic-slice_fusion.6
  77.4 0.6 fusion.117
  78.1 0.6 compare_bitcast_fusion.2
  80.9 0.7 dynamic_slice.31
  82.2 0.9 constant_dynamic-slice_fusion.6
  83.4 0.6 fusion.117
  84.0 0.6 compare_bitcast_fusion.2
  86.8 0.7 dynamic_slice.31
  88.1 0.9 constant_dynamic-slice_fusion.6
  89.3 0.6 fusion.117
  92.8 0.7 dynamic_slice.31
  94.1 0.9 constant_dynamic-slice_fusion.6
  95.3 0.6 fusion.117
  98.7 0.7 dynamic_slice.31
  100.0 0.9 constant_dynamic-slice_fusion.6
  101.2 0.6 fusion.117
  104.7 0.7 dynamic_slice.31
  106.0 0.9 constant_dynamic-slice_fusion.6
  107.2 0.6 fusion.117
  107.8 0.6 compare_bitcast_fusion.2
  110.8 2.3 %all-gather.2 = f32[8,128,128]{2,1,0:T(8,128)S(1)} all-gather(f32[4,128,128]{2,1,0:T(8,128)S(1)} %get-tuple-element.130), channel_id=4, replica_groups=mesh['seq_0'=8,'seq_1'=2,'kv'=8,'dp'=4] {'seq_1'}, dimensions={0}, use_global_device_ids=true | all-gather | bytes 786432 | tf_op jit(solution)/shard_map/all_gather | solution.py:52
  113.1 1.8 all-reduce
  119.1 0.7 fusion.34
  119.9 1.3 dynamic-slice.1
  124.9 13.5 %all-reduce.1 = s32[16]{0:T(128)S(1)} all-reduce(s32[16]{0:T(128)S(1)} %fusion.99), channel_id=3, replica_groups=mesh['seq_0'=8,'seq_1'=2,'kv'=8,'dp'=4] {'seq_0'}, use_global_device_ids=true, to_apply=%add.1 | all-reduce | flops 16 | bytes 128
  138.5 0.7 fusion.104
  161.6 9.0 %all-gather.8.cloned.1.call-done = f32[8,4,128,128]{3,2,1,0:T(8,128)} async-done(((f32[1,4,128,128]{3,2,1,0:T(8,128)}), f32[8,4,128,128]{3,2,1,0:T(8,128)}) %all-gather.8.cloned.1.call-update) | async-done | bytes 2097168 | tf_op jit(solution)/shard_map/all_gather | solution.py:52
  170.5 2.6 %multiply_reduce_fusion = (f32[128,4,4]{0,2,1:T(4,128)S(1)}, f32[128,4,4,128]{0,3,2,1:T(8,128)S(1)}) fusion(bf16[128,4,4,128]{0,3,2,1:T(8,128)(2,1)S(1)} %bitcast.202, f32[8,4,128,128]{3,2,1,0:T(8,128)} %all-gather.8.cloned.1.call-done, f32[8,128,128]{2,1,0:T(8,128)S(1)} %all-gather.2, pred[]{:T(512)S(6)} %lt.43, pred[]{:T(512)S(6)} %and.43, pred[]{:T(512)S(6)} %gt.31, ...), kind=kOutput, calls=%fused_computation.31 | convolution fusion | flops 405993472 | bytes 4202654 | tf_op jit(solution)/shard_map/rgqd,gde->rgqe/dot_general | solution.py:205
  173.7 1.3 copy.52
  (92 shorter events, 9.1 us)
Async XLA Ops:
  6.5 52.2 %all-gather.6.cloned.1.call-start = ((), (), s32[]{:S(2)}) async-start(), calls=%async_computation.1 | async-start | bytes 2359296 | tf_op jit(solution)/shard_map/all_gather | solution.py:17
  9.5 51.9 %all-to-all-start = ((s32[8,1,128]{2,1,0:T(1,128)}), s32[8,1,128]{2,1,0:T(1,128)S(1)}, u32[]{:S(2)}, u32[]{:S(2)}) async-start(s32[8,1,128]{2,1,0:T(1,128)} %stack.2), calls=%async_computation | async-start | bytes 8192 | tf_op jit(solution)/shard_map/all_to_all | solution.py:155
  19.8 150.7 %all-gather.8.cloned.1.call-start = ((), (), s32[]{:S(2)}) async-start(), calls=%async_computation.2 | async-start | bytes 2359296 | tf_op jit(solution)/shard_map/all_gather | solution.py:52
  21.2 40.2 %copy-start = (bf16[128,2048]{0,1:T(8,128)(2,1)}, bf16[128,2048]{0,1:T(8,128)(2,1)S(1)}, u32[]{:S(2)}) copy-start(bf16[128,2048]{0,1:T(8,128)(2,1)S(1)} %copy.45) | copy-start | bytes 1572868
  23.5 38.0 %copy-start.2 = (s32[128]{0:T(128)S(1)}, s32[128]{0:T(128)}, u32[]{:S(2)}) copy-start(s32[128]{0:T(128)} %param.13) | copy-start | bytes 1540
  61.5 60.4 %copy-start.4 = (f32[16]{0:T(128)S(1)}, f32[16]{0:T(128)}, u32[]{:S(2)}) copy-start(f32[16]{0:T(128)} %param.14) | copy-start | bytes 196
  110.8 59.8 %copy-start.1 = (bf16[128,2048]{0,1:T(8,128)(2,1)S(1)}, bf16[128,2048]{0,1:T(8,128)(2,1)}, u32[]{:S(2)}) copy-start(bf16[128,2048]{0,1:T(8,128)(2,1)} %copy-done) | copy-start | bytes 1572868
  161.6 11.6 %copy-start.3 = (f32[2048]{0:T(1024)S(1)}, f32[2048]{0:T(1024)}, u32[]{:S(2)}) copy-start(f32[2048]{0:T(1024)} %param.15) | copy-start | bytes 24580
Sparse Core Ops, SparseCore 0:
  9.4 49.2 all-gather.5
  120.0 50.5 all-gather.7
